TPU v7x, 32 devices: a whole 2x2x4 slice. The times are simulated.
32 devices in a mesh: groups: 2 (over y), blk: 4 (over z), cols: 2 (over x), sub: 2 (over core).
Axes of the slice: x: 2, y: 2, z: 4, core: 2. Of those that a mesh axis runs over, the one named last changes fastest.
Arguments:
- features: bfloat16 [4096, 256], P(('groups', 'blk', 'cols'), 'sub'), parts along dimension 0, may hold values from -60 to 60, as said below
- vector: float32 [4096], P(('groups', 'blk', 'cols')), parts along dimension 0, may hold values from 0.1 to 100, as said below
Outputs:
- new_vector: float32 [4096], P(('groups', 'blk', 'cols')), parts along dimension 0
- mean_affinity: float32 [4096], P(('groups', 'blk', 'cols')), parts along dimension 0
There are 2 independent parts, one for each index of `groups`. A program takes and returns all parts, laid end to end along the dimension named above; each array names one. Nothing has to cross between parts.
Inputs may be any that keep to these rules, and one draw needn't show every extreme that they name: Real-valued features; no row is zero. `vector`: positive entries.
All inputs are finite; a program needn't handle non-finite values. Where the computation divides by a largest or mean magnitude, that divisor is 1e-20 or more.
Results may differ from a plain program's by a relative error of at most 0.0033.
Values may be sent and summed in bfloat16 or wider, within the bound.
A program may use at most 64 MiB of HBM per device.

v0:
```python
import math

import jax
import jax.numpy as jnp
from jax import lax
from jax.sharding import PartitionSpec as P

POWER = 16


def fold_block(row_feats, totals, col_feats, col_vals):
    cosine = lax.dot_general(
        row_feats, col_feats, (((1,), (1,)), ((), ())), preferred_element_type=jnp.float32
    )
    affinity = (1.0 + cosine) * 0.5
    for level in range(POWER.bit_length() - 1):
        affinity = affinity * affinity
    weighted = totals[0] + jnp.dot(affinity, col_vals, precision=lax.Precision.HIGHEST)
    degree = totals[1] + jnp.sum(affinity, axis=1)
    return (weighted, degree)


def sweep(row_feats, totals, pieces):
    col_feats, col_vals = pieces
    columns = col_feats.shape[0]
    block_len = math.gcd(columns, 512)
    blocks = columns // block_len
    if blocks == 1:
        return fold_block(row_feats, totals, col_feats, col_vals)
    stacked = (
        col_feats.reshape(blocks, block_len, col_feats.shape[1]),
        col_vals.reshape(blocks, block_len),
    )

    def advance(running, member):
        return (fold_block(row_feats, running, member[0], member[1]), None)

    result, unused = lax.scan(advance, totals, stacked)
    return result


def empty_sums(length):
    return (jnp.zeros((length,), jnp.float32), jnp.zeros((length,), jnp.float32))


def local(features, vector):
    own_rows = features.shape[0]
    half_rows = own_rows // 2
    gathered = lax.all_gather(features, "sub", axis=1, tiled=True)
    widened = gathered.astype(jnp.float32)
    unit_rows = (
        widened
        * lax.rsqrt(jnp.mean(widened * widened, axis=1, keepdims=True) + 1e-06)
        * (1.0 / math.sqrt(widened.shape[1]))
    ).astype(jnp.bfloat16)
    sub_index = lax.axis_index("sub")
    col_feats = lax.dynamic_slice_in_dim(unit_rows, sub_index * half_rows, half_rows, 0)
    col_vals = lax.dynamic_slice_in_dim(vector, sub_index * half_rows, half_rows, 0)
    points = own_rows * lax.axis_size("blk") * lax.axis_size("cols")
    block_feats = lax.all_gather(unit_rows, "cols", axis=0, tiled=True)
    partial_sums = sweep(
        block_feats,
        empty_sums(block_feats.shape[0]),
        (
            lax.all_gather(col_feats, "blk", axis=0, tiled=True),
            lax.all_gather(col_vals.astype(jnp.bfloat16), "blk", axis=0, tiled=True).astype(
                jnp.float32
            ),
        ),
    )
    block_weighted, block_degree = lax.psum((partial_sums[0], partial_sums[1]), ("cols", "sub"))
    block_averaged = block_weighted / block_degree
    total = lax.psum(jnp.sum(jnp.abs(block_averaged)), "blk")
    first_row = lax.axis_index("cols") * own_rows
    averaged = lax.dynamic_slice_in_dim(block_averaged, first_row, own_rows, 0)
    degree = lax.dynamic_slice_in_dim(block_degree, first_row, own_rows, 0)
    mean_abs = total / points + 1e-06
    return (averaged / mean_abs, degree / points)


def solution(mesh):
    in_specs = (P(("groups", "blk", "cols"), "sub"), P(("groups", "blk", "cols")))
    out_specs = (P(("groups", "blk", "cols")), P(("groups", "blk", "cols")))
    return jax.shard_map(local, mesh=mesh, in_specs=in_specs, out_specs=out_specs, check_vma=False)
```

profile of v0, /device:TPU:0, one launch (start us, length us, event | category | flops | bytes accessed | tf_op | source)
XLA Modules:
  0.0 53.8 jit_solution(12219842867503228828)
XLA Ops:
  0.6 0.0 copy-start
  0.7 2.3 %all_gather.12 = bf16[256,256]{1,0:T(8,128)(2,1)S(1)} all-gather(bf16[256,128]{1,0:T(8,128)(2,1)} %param.2), channel_id=1, replica_groups=mesh['groups'=2,'blk'=4,'cols'=2,'sub'=2] {'sub'}, dimensions={1}, use_global_device_ids=true | all-gather | bytes 196608 | tf_op jit(solution)/shard_map/all_gather | solution.py:49
  2.9 0.1 fusion.5
  3.1 0.1 fusion.7
  3.2 15.4 %all_gather.14 = bf16[512,256]{1,0:T(8,128)(2,1)S(1)} all-gather(bf16[128,256]{1,0:T(8,128)(2,1)S(1)} %constant_dynamic-slice_fusion), channel_id=1, replica_groups=mesh['groups'=2,'blk'=4,'cols'=2,'sub'=2] {'blk'}, dimensions={0}, use_global_device_ids=true | all-gather | bytes 327680 | tf_op jit(solution)/shard_map/all_gather | solution.py:65
  18.6 5.6 %all_gather.13 = bf16[512,256]{1,0:T(8,128)(2,1)S(1)} all-gather(bf16[256,256]{1,0:T(8,128)(2,1)S(1)} %fusion.7), channel_id=1, replica_groups=mesh['groups'=2,'blk'=4,'cols'=2,'sub'=2] {'cols'}, dimensions={0}, use_global_device_ids=true | all-gather | bytes 393216 | tf_op jit(solution)/shard_map/all_gather | solution.py:60
  24.2 0.4 fusion.10
  24.6 0.0 copy-done
  24.6 0.1 convert_bitcast_fusion
  24.7 11.5 %all-gather = bf16[4,1,128]{2,1,0:T(2,128)(2,1)S(1)} all-gather(bf16[1,1,128]{2,1,0:T(2,128)(2,1)S(1)} %convert_bitcast_fusion), channel_id=1, replica_groups=mesh['groups'=2,'blk'=4,'cols'=2,'sub'=2] {'blk'}, dimensions={0}, use_global_device_ids=true | all-gather | bytes 1280 | tf_op jit(solution)/shard_map/all_gather | solution.py:66
  36.2 0.4 fusion.8
  36.7 5.6 %all-reduce = (f32[512]{0:T(512)S(1)}, f32[512]{0:T(512)S(1)}) all-reduce(f32[512]{0:T(512)S(1)} %bitcast.9, f32[512]{0:T(512)S(1)} %get-tuple-element.6), channel_id=1, replica_groups=mesh['groups'=2,'blk'=4,'cols'=2,'sub'=2] {'cols','sub'}, use_global_device_ids=true, to_apply=%region_1.0 | all-reduce | flops 1024 | bytes 8192 | tf_op jit(solution)/shard_map/psum | solution.py:71
  42.3 0.6 %dynamic-slice_multiply_fusion = f32[256]{0:T(256)} fusion(f32[512]{0:T(512)S(1)} %get-tuple-element.3, s32[]{:T(128)S(6)} %select_n.9), kind=kLoop, calls=%fused_computation.14 | loop fusion | flops 256 | bytes 2052 | tf_op jit(solution)/shard_map/div | solution.py:78
  43.0 0.6 %abs_reduce_fusion = (f32[]{:T(128)}, f32[512]{0:T(512)S(1)}) fusion(f32[512]{0:T(512)S(1)} %get-tuple-element.2, f32[512]{0:T(512)S(1)} %get-tuple-element.3), kind=kLoop, calls=%fused_computation.13 | loop fusion | flops 1535 | bytes 6148 | tf_op jit(solution)/shard_map/reduce_sum | solution.py:73
  43.6 9.0 %psum.23 = f32[]{:T(128)} all-reduce(f32[]{:T(128)} %get-tuple-element.4), channel_id=1, replica_groups=mesh['groups'=2,'blk'=4,'cols'=2,'sub'=2] {'blk'}, use_global_device_ids=true, to_apply=%region_5.0 | all-reduce | flops 1 | bytes 8 | tf_op jit(solution)/shard_map/psum | solution.py:73
  53.2 0.6 %dynamic-slice_divide_fusion = f32[256]{0:T(256)} fusion(f32[512]{0:T(512)S(1)} %get-tuple-element.5, s32[]{:T(128)S(6)} %select_n.9, f32[]{:T(128)S(6)} %add.40), kind=kLoop, calls=%fused_computation.15 | loop fusion | flops 256 | bytes 2056 | tf_op jit(solution)/shard_map/div | solution.py:78
  (2 shorter events, 0.0 us)
Async XLA Ops:
  0.6 24.0 %copy-start = (f32[256]{0:T(256)S(1)}, f32[256]{0:T(256)}, u32[]{:S(2)}) copy-start(f32[256]{0:T(256)} %param.3) | copy-start | bytes 3076
where the time goes:
time: 54.1 us; the launch traced here: 53.8 us
  blocking collectives  49.4 us (91%)
  other arithmetic  2.11 us (4%)
  between operations  1.34 us (2%)
  matrix products  0.89 us (2%)
    all_gather x1, blocking collectives, local(): lax.all_gather(col_feats, 'blk', axis=0, tiled=True)  15.4 us
    all_gather x1, blocking collectives, local(): lax.all_gather(col_vals.astype(jnp.bfloat16), 'blk', axis=0, tiled=True)  11.5 us
    psum x1, blocking collectives, local(): total = lax.psum(jnp.sum(jnp.abs(block_averaged)), 'blk')  8.97 us
    psum x1, blocking collectives, local(): lax.psum((partial_sums[0], partial_sums[1]), ('cols', 'sub'))  5.64 us
    all_gather x1, blocking collectives, local(): block_feats = lax.all_gather(unit_rows, 'cols', axis=0, tiled=True)  5.62 us
    all_gather x1, blocking collectives, local(): gathered = lax.all_gather(features, 'sub', axis=1, tiled=True)  2.28 us
    div x2, other arithmetic, local(): return (averaged / mean_abs, degree / points)  1.28 us

commit v1 on v0

v1 whole, which is shorter than its diff:
```python
import functools
import math

import jax
import jax.numpy as jnp
from jax import lax
from jax.experimental import pallas as pl
from jax.experimental.pallas import tpu as pltpu
from jax.sharding import PartitionSpec as P

POWER = 16
MESH = pl.DeviceIdType.MESH


def normalize(first, second):
    first = first.astype(jnp.float32)
    second = second.astype(jnp.float32)
    width = first.shape[1] + second.shape[1]
    squares = jnp.sum(first * first + second * second, axis=1, keepdims=True)
    scale = lax.rsqrt(squares * (1.0 / width) + 1e-06) * (1.0 / math.sqrt(width))
    return (first * scale).astype(jnp.bfloat16), (second * scale).astype(jnp.bfloat16)


def kernel(
    nb, nc, ns, f_ref, v_ref, new_ref, mean_ref,
    row_buf, col_buf, val_buf, unit, part, red_buf, tot, tot_buf,
    row_send, row_recv, col_send, col_recv, val_send, val_recv,
    red_send, red_recv, tot_send, tot_recv,
):
    z, x, c = lax.axis_index("blk"), lax.axis_index("cols"), lax.axis_index("sub")
    rows, feats = f_ref.shape
    half = rows // ns
    points = rows * nb * nc
    plane = [(d, e) for d in range(nc) for e in range(ns) if (d, e) != (0, 0)]
    ahead = list(range(1, nb))

    def plane_id(d, e):
        return {"cols": lax.rem(x + d, nc), "sub": lax.rem(c + e, ns)}

    def line_id(d, e):
        return {"blk": lax.rem(z + d, nb), "sub": lax.rem(c + e, ns)}

    barrier = pltpu.get_barrier_semaphore()
    for d in ahead:
        for e in range(ns):
            pl.semaphore_signal(barrier, 1, device_id=line_id(d, e), device_id_type=MESH)
    for d, e in plane:
        pl.semaphore_signal(barrier, 1, device_id=plane_id(d, e), device_id_type=MESH)
    pl.semaphore_wait(barrier, len(plane) + len(ahead) * ns)

    def remote(src, dst, send, recv, device):
        copy = pltpu.make_async_remote_copy(
            src_ref=src, dst_ref=dst, send_sem=send, recv_sem=recv,
            device_id=device, device_id_type=MESH,
        )
        copy.start()
        return copy

    row_copy, col_copy, val_copy, red_copy, tot_copy = {}, {}, {}, {}, {}
    own = pl.ds(pl.multiple_of(c * half, half), half)
    for d, e in plane:
        slot = ((nc - d) % nc, e)
        row_copy[slot] = remote(
            f_ref, row_buf.at[slot], row_send.at[slot], row_recv.at[slot], plane_id(d, e)
        )
    for d in ahead:
        val_copy[nb - d] = remote(
            v_ref.at[:, own], val_buf.at[nb - d], val_send.at[nb - d], val_recv.at[nb - d],
            line_id(d, 0),
        )
        for e in range(ns):
            slot = (nb - d, e)
            wanted = pl.ds(pl.multiple_of(lax.rem(c + e, ns) * half, half), half)
            col_copy[slot] = remote(
                f_ref.at[wanted, :], col_buf.at[slot], col_send.at[slot], col_recv.at[slot],
                line_id(d, e),
            )

    for d in range(nc):
        for e in range(ns):
            if (d, e) in row_copy:
                row_copy[d, e].wait_recv()
        mine = f_ref[...] if d == 0 else row_buf[d, 0]
        near, far = normalize(mine, row_buf[d, 1])
        unit[pl.ds(d * rows, rows), :feats] = near
        unit[pl.ds(d * rows, rows), feats:] = far

    def fold(col_feats, values):
        cosine = lax.dot_general(
            col_feats, unit[...], (((1,), (1,)), ((), ())), preferred_element_type=jnp.float32
        )
        affinity = (1.0 + cosine) * 0.5
        for level in range(POWER.bit_length() - 1):
            affinity = affinity * affinity
        tall = jnp.broadcast_to(values, (128, half)).T[:, :1]
        return (
            jnp.sum(affinity * tall, axis=0, keepdims=True),
            jnp.sum(affinity, axis=0, keepdims=True),
        )

    weighted, degree = fold(unit[own, :], v_ref[:, own])
    for d in sorted(ahead, key=lambda d: min(d, nb - d)):
        for e in range(ns):
            col_copy[d, e].wait_recv()
        val_copy[d].wait_recv()
        near, far = normalize(col_buf[d, 0], col_buf[d, 1])
        more, extra = fold(jnp.concatenate([near, far], axis=1), val_buf[d])
        weighted, degree = weighted + more, degree + extra
    for d in range(nc):
        place = lax.rem(x + d, nc)
        part[place, 0:1, :] = weighted[:, d * rows:(d + 1) * rows]
        part[place, 1:2, :] = degree[:, d * rows:(d + 1) * rows]

    for d, e in plane:
        slot = ((nc - d) % nc, e)
        red_copy[slot] = remote(
            part, red_buf.at[slot], red_send.at[slot], red_recv.at[slot], plane_id(d, e)
        )
    for slot in plane:
        red_copy[slot].wait_recv()

    def gathered(place):
        total = None
        for d in range(nc):
            first = part[place] if d == 0 else red_buf[d, 0, place]
            pair = first + red_buf[d, 1, place]
            total = pair if total is None else total + pair
        return total[0:1, :], total[1:2, :]

    lanes = jnp.zeros((1, 128), jnp.float32)
    for place in range(nc):
        block_weighted, block_degree = gathered(place)
        size = jnp.abs(block_weighted / block_degree)
        for start in range(0, rows, 128):
            lanes = lanes + size[:, start:start + 128]
    tot[...] = lanes
    for d in ahead:
        tot_copy[nb - d] = remote(
            tot, tot_buf.at[nb - d], tot_send.at[nb - d], tot_recv.at[nb - d], line_id(d, 0)
        )
    own_weighted, own_degree = gathered(x)
    averaged = own_weighted / own_degree
    mean_ref[...] = own_degree / points
    for copies in (row_copy, col_copy, val_copy, red_copy):
        for copy in copies.values():
            copy.wait_send()
    for d in ahead:
        tot_copy[d].wait_recv()
        lanes = lanes + tot_buf[d]
    total = jnp.sum(lanes, axis=1, keepdims=True)
    new_ref[...] = averaged / (total / points + 1e-06)
    for copy in tot_copy.values():
        copy.wait_send()


def local(nb, nc, ns, features, vector):
    rows, feats = features.shape
    half = rows // ns
    dma = pltpu.SemaphoreType.DMA
    vmem = pl.BlockSpec(memory_space=pltpu.VMEM)
    new, mean = pl.pallas_call(
        functools.partial(kernel, nb, nc, ns),
        out_shape=(
            jax.ShapeDtypeStruct((1, rows), jnp.float32),
            jax.ShapeDtypeStruct((1, rows), jnp.float32),
        ),
        in_specs=[vmem, vmem],
        out_specs=(vmem, vmem),
        scratch_shapes=[
            pltpu.VMEM((nc, ns, rows, feats), jnp.bfloat16),
            pltpu.VMEM((nb, ns, half, feats), jnp.bfloat16),
            pltpu.VMEM((nb, 1, half), jnp.float32),
            pltpu.VMEM((nc * rows, ns * feats), jnp.bfloat16),
            pltpu.VMEM((nc, 2, rows), jnp.float32),
            pltpu.VMEM((nc, ns, nc, 2, rows), jnp.float32),
            pltpu.VMEM((1, 128), jnp.float32),
            pltpu.VMEM((nb, 1, 128), jnp.float32),
            dma((nc, ns)), dma((nc, ns)),
            dma((nb, ns)), dma((nb, ns)),
            dma((nb,)), dma((nb,)),
            dma((nc, ns)), dma((nc, ns)),
            dma((nb,)), dma((nb,)),
        ],
        compiler_params=pltpu.CompilerParams(collective_id=0, has_side_effects=True),
    )(features, vector.reshape(1, rows))
    return new.reshape(rows), mean.reshape(rows)


def solution(mesh):
    in_specs = (P(("groups", "blk", "cols"), "sub"), P(("groups", "blk", "cols")))
    out_specs = (P(("groups", "blk", "cols")), P(("groups", "blk", "cols")))
    sizes = (mesh.shape["blk"], mesh.shape["cols"], mesh.shape["sub"])
    return jax.shard_map(
        functools.partial(local, *sizes), mesh=mesh, in_specs=in_specs, out_specs=out_specs,
        check_vma=False,
    )
```

time: 54.1 us -> 24.1 us (0.45)
  blocking collectives: 49.4 us -> 0 us
  Pallas kernels: 0 us -> 21.4 us
  other arithmetic: 2.11 us -> 0 us
  local copies, waits for them, and re-layouts: 0.1 us -> 1.86 us
  matrix products: 0.89 us -> 0 us
  between operations: 1.34 us -> 0.65 us
    all_gather x4 -> x0, blocking collectives: 34.8 us -> none  [the longest x1 15.4 us: local(): lax.all_gather(col_feats, 'blk', axis=0, tiled=True)]
    pallas_call x0 -> x1, Pallas kernels: none -> 21.4 us  [local(): pl.pallas_call(functools.partial(kernel, nb, nc, ns), out_shape=(jax.Shap...]
    psum x2 -> x0, blocking collectives: 14.6 us -> none  [the longest x1 8.97 us: local(): total = lax.psum(jnp.sum(jnp.abs(block_averaged)), 'blk')]
    unnamed x3 -> x6, local copies, waits for them, and re-layouts: 0.09 us -> 1.86 us
    div x2 -> x0, other arithmetic: 1.28 us -> none  [local(): return (averaged / mean_abs, degree / points)]
    dot_general x2 -> x0, matrix products: 0.89 us -> none  [the longest x1 0.45 us: fold_block(): jnp.dot(affinity, col_vals, precision=lax.Precision.HIGHEST)]
    reduce_sum x2 -> x0, other arithmetic: 0.72 us -> none  [the longest x1 0.61 us: local(): total = lax.psum(jnp.sum(jnp.abs(block_averaged)), 'blk')]
where the time goes in v1:
time: 24.1 us; the launch traced here: 23.9 us
  Pallas kernels  21.4 us (89%)
  local copies, waits for them, and re-layouts  1.86 us (8%)
  between operations  0.65 us (3%)
    pallas_call x1, Pallas kernels, local(): pl.pallas_call(functools.partial(kernel, nb, nc, ns), out_shape=(jax.Shap...  21.4 us
    unnamed x6, local copies, waits for them, and re-layouts  1.86 us

profile of v1, /device:TPU:0, one launch (start us, length us, event | category | flops | bytes accessed | tf_op | source)
XLA Modules:
  0.0 23.9 jit_solution(17977986667092095758)
XLA Ops:
  0.6 21.4 %shard_map.41 = (f32[1,256]{1,0:T(1,128)}, f32[1,256]{1,0:T(1,128)}) custom-call(bf16[256,128]{1,0:T(8,128)(2,1)} %f_ref.1, f32[1,256]{1,0:T(1,128)} %bitcast.3), custom_call_target="tpu_custom_call" | custom-call | tf_op jit(solution)/shard_map/pallas_call | solution.py:161
  22.1 0.0 copy-start.1
  22.1 0.7 %copy-done.1 = f32[1,256]{1,0:T(1,128)S(1)} copy-done((f32[1,256]{1,0:T(1,128)S(1)}, f32[1,256]{1,0:T(1,128)}, u32[]{:S(2)}) %copy-start.1) | copy-done | bytes 1048
  22.7 0.0 copy-start
  22.7 0.6 %copy.6 = f32[256]{0:T(256)} copy(f32[256]{0:T(256)S(1)} %bitcast.5) | data formatting | bytes 2048
  23.3 0.1 copy-done
  23.4 0.6 %copy.7 = f32[256]{0:T(256)} copy(f32[256]{0:T(256)S(1)} %bitcast.4) | data formatting | bytes 2048
Async XLA Ops:
  22.1 0.7 %copy-start.1 = (f32[1,256]{1,0:T(1,128)S(1)}, f32[1,256]{1,0:T(1,128)}, u32[]{:S(2)}) copy-start(f32[1,256]{1,0:T(1,128)} %get-tuple-element.4) | copy-start | bytes 3076
  22.7 0.6 %copy-start = (f32[1,256]{1,0:T(1,128)S(1)}, f32[1,256]{1,0:T(1,128)}, u32[]{:S(2)}) copy-start(f32[1,256]{1,0:T(1,128)} %get-tuple-element.5) | copy-start | bytes 3076

commit v2 on v1

v2 whole, which is shorter than its diff:
```python
import functools
import math

import jax
import jax.numpy as jnp
from jax import lax
from jax.experimental import pallas as pl
from jax.experimental.pallas import tpu as pltpu
from jax.sharding import PartitionSpec as P

POWER = 16
MESH = pl.DeviceIdType.MESH


def normalize(first, second):
    first = first.astype(jnp.float32)
    second = second.astype(jnp.float32)
    width = first.shape[1] + second.shape[1]
    squares = jnp.sum(first * first + second * second, axis=1, keepdims=True)
    scale = lax.rsqrt(squares * (1.0 / width) + 1e-06) * (1.0 / math.sqrt(width))
    return (first * scale).astype(jnp.bfloat16), (second * scale).astype(jnp.bfloat16)


def kernel(
    nb, nc, ns, f_ref, v_ref, new_ref, mean_ref,
    row_buf, col_buf, val_buf, unit, part, all_buf, own_sums,
    row_send, row_recv, col_send, col_recv, val_send, val_recv,
    all_send, all_recv, below_in, above_in,
):
    z, x, c = lax.axis_index("blk"), lax.axis_index("cols"), lax.axis_index("sub")
    rows, feats = f_ref.shape
    half = rows // ns
    points = rows * nb * nc
    plane = [(d, e) for d in range(nc) for e in range(ns) if (d, e) != (0, 0)]
    ahead = list(range(1, nb))

    def plane_id(d, e):
        return {"cols": lax.rem(x + d, nc), "sub": lax.rem(c + e, ns)}

    def line_id(d, e):
        return {"blk": lax.rem(z + d, nb), "sub": lax.rem(c + e, ns)}

    def full_id(dz, d, e):
        return {
            "blk": lax.rem(z + dz, nb), "cols": lax.rem(x + d, nc), "sub": lax.rem(c + e, ns),
        }

    barrier = pltpu.get_barrier_semaphore()
    for cond, d in ((z + 1 < nb, 1), (z >= 1, nb - 1)):
        @pl.when(cond)
        def _():
            for e in range(ns):
                pl.semaphore_signal(barrier, 1, device_id=line_id(d, e), device_id_type=MESH)
    for d, e in plane:
        pl.semaphore_signal(barrier, 1, device_id=plane_id(d, e), device_id_type=MESH)
    beside = jnp.where(z >= 1, ns, 0) + jnp.where(z + 1 < nb, ns, 0)
    pl.semaphore_wait(barrier, len(plane) + beside)

    def remote(src, dst, send, recv, device):
        return pltpu.make_async_remote_copy(
            src_ref=src, dst_ref=dst, send_sem=send, recv_sem=recv,
            device_id=device, device_id_type=MESH,
        )

    row_copy, col_copy, val_copy, all_copy = {}, {}, {}, {}
    own = pl.ds(pl.multiple_of(c * half, half), half)
    for d in ahead:
        val_copy[nb - d] = remote(
            v_ref.at[:, own], val_buf.at[nb - d], val_send.at[nb - d], val_recv.at[nb - d],
            line_id(d, 0),
        )
        for e in range(ns):
            slot = (nb - d, e)
            wanted = pl.ds(pl.multiple_of(lax.rem(c + e, ns) * half, half), half)
            col_copy[slot] = remote(
                f_ref.at[wanted, :], col_buf.at[slot], col_send.at[slot], col_recv.at[slot],
                line_id(d, e),
            )

    def start_line(d):
        for e in range(ns):
            col_copy[nb - d, e].start()
        val_copy[nb - d].start()

    for k in ahead:
        @pl.when(z + k < nb)
        def _():
            if k > 1:
                pl.semaphore_wait(above_in.at[k], 1)
            if k + 1 < nb:
                @pl.when(z >= 1)
                def _():
                    pl.semaphore_signal(
                        above_in.at[k + 1], 1, device_id=line_id(nb - 1, 0), device_id_type=MESH
                    )
            start_line(k)

        @pl.when(z >= k)
        def _():
            if k > 1:
                pl.semaphore_wait(below_in.at[k], 1)
            if k + 1 < nb:
                @pl.when(z + 1 < nb)
                def _():
                    pl.semaphore_signal(
                        below_in.at[k + 1], 1, device_id=line_id(1, 0), device_id_type=MESH
                    )
            start_line(nb - k)

        if k == 1:
            for d, e in plane:
                slot = ((nc - d) % nc, e)
                row_copy[slot] = remote(
                    f_ref, row_buf.at[slot], row_send.at[slot], row_recv.at[slot], plane_id(d, e)
                )
                row_copy[slot].start()

    for d in range(nc):
        for e in range(ns):
            if (d, e) in row_copy:
                row_copy[d, e].wait_recv()
        mine = f_ref[...] if d == 0 else row_buf[d, 0]
        near, far = normalize(mine, row_buf[d, 1])
        place = pl.ds(pl.multiple_of(lax.rem(x + d, nc) * rows, rows), rows)
        unit[place, :feats] = near
        unit[place, feats:] = far

    def fold(col_feats, values):
        cosine = lax.dot_general(
            col_feats, unit[...], (((1,), (1,)), ((), ())), preferred_element_type=jnp.float32
        )
        affinity = (1.0 + cosine) * 0.5
        for level in range(POWER.bit_length() - 1):
            affinity = affinity * affinity
        tall = jnp.broadcast_to(values, (128, half)).T[:, :1]
        return (
            jnp.sum(affinity * tall, axis=0, keepdims=True),
            jnp.sum(affinity, axis=0, keepdims=True),
        )

    own_cols = pl.ds(pl.multiple_of(x * rows + c * half, half), half)
    weighted, degree = fold(unit[own_cols, :], v_ref[:, own])
    for d in sorted(ahead, key=lambda d: min(d, nb - d)):
        for e in range(ns):
            col_copy[d, e].wait_recv()
        val_copy[d].wait_recv()
        near, far = normalize(col_buf[d, 0], col_buf[d, 1])
        more, extra = fold(jnp.concatenate([near, far], axis=1), val_buf[d])
        weighted, degree = weighted + more, degree + extra
    tiles = nc * rows // 128
    for i in range(tiles):
        part[i:i + 1, :] = weighted[:, i * 128:(i + 1) * 128]
        part[tiles + i:tiles + i + 1, :] = degree[:, i * 128:(i + 1) * 128]

    for dz in ahead + [0]:
        for d in range(nc):
            for e in range(ns):
                if (dz, d, e) == (0, 0, 0):
                    continue
                slot = ((nb - dz) % nb, (nc - d) % nc, e)
                all_copy[slot] = remote(
                    part, all_buf.at[slot], all_send.at[slot], all_recv.at[slot],
                    full_id(dz, d, e),
                )
                all_copy[slot].start()
    for copies in (row_copy, col_copy, val_copy):
        for copy in copies.values():
            copy.wait_send()

    sizes = None
    for dz in range(nb):
        total = None
        for d in range(nc):
            for e in range(ns):
                if (dz, d, e) != (0, 0, 0):
                    all_copy[dz, d, e].wait_recv()
            first = part[...] if (dz, d) == (0, 0) else all_buf[dz, d, 0]
            pair = first + all_buf[dz, d, 1]
            total = pair if total is None else total + pair
        averaged = total[:tiles] / total[tiles:]
        if dz == 0:
            own_sums[:tiles] = averaged
            own_sums[tiles:] = total[tiles:]
        size = jnp.abs(averaged)
        sizes = size if sizes is None else sizes + size
    mean = jnp.sum(sizes, axis=(0, 1), keepdims=True) / points + 1e-06
    for i in range(rows // 128):
        lanes = slice(i * 128, (i + 1) * 128)
        first = x * (rows // 128) + i
        new_ref[:, lanes] = own_sums[pl.ds(first, 1), :] / mean
        mean_ref[:, lanes] = own_sums[pl.ds(tiles + first, 1), :] / points
    for copy in all_copy.values():
        copy.wait_send()


def local(nb, nc, ns, features, vector):
    rows, feats = features.shape
    half = rows // ns
    tiles = 2 * nc * rows // 128
    dma = pltpu.SemaphoreType.DMA
    vmem = pl.BlockSpec(memory_space=pltpu.VMEM)
    new, mean = pl.pallas_call(
        functools.partial(kernel, nb, nc, ns),
        out_shape=(
            jax.ShapeDtypeStruct((1, rows), jnp.float32),
            jax.ShapeDtypeStruct((1, rows), jnp.float32),
        ),
        in_specs=[vmem, vmem],
        out_specs=(vmem, vmem),
        scratch_shapes=[
            pltpu.VMEM((nc, ns, rows, feats), jnp.bfloat16),
            pltpu.VMEM((nb, ns, half, feats), jnp.bfloat16),
            pltpu.VMEM((nb, 1, half), jnp.float32),
            pltpu.VMEM((nc * rows, ns * feats), jnp.bfloat16),
            pltpu.VMEM((tiles, 128), jnp.float32),
            pltpu.VMEM((nb, nc, ns, tiles, 128), jnp.float32),
            pltpu.VMEM((tiles, 128), jnp.float32),
            dma((nc, ns)), dma((nc, ns)),
            dma((nb, ns)), dma((nb, ns)),
            dma((nb,)), dma((nb,)),
            dma((nb, nc, ns)), dma((nb, nc, ns)),
            pltpu.SemaphoreType.REGULAR((nb,)), pltpu.SemaphoreType.REGULAR((nb,)),
        ],
        compiler_params=pltpu.CompilerParams(collective_id=0, has_side_effects=True),
    )(features, vector.reshape(1, rows))
    return new.reshape(rows), mean.reshape(rows)


def solution(mesh):
    in_specs = (P(("groups", "blk", "cols"), "sub"), P(("groups", "blk", "cols")))
    out_specs = (P(("groups", "blk", "cols")), P(("groups", "blk", "cols")))
    sizes = (mesh.shape["blk"], mesh.shape["cols"], mesh.shape["sub"])
    return jax.shard_map(
        functools.partial(local, *sizes), mesh=mesh, in_specs=in_specs, out_specs=out_specs,
        check_vma=False,
    )
```

time: 24.1 us -> 21.5 us (0.89)
  Pallas kernels: 21.4 us -> 18.8 us
    pallas_call x1, Pallas kernels: 21.4 us -> 18.8 us  [local(): pl.pallas_call(functools.partial(kernel, nb, nc, ns), out_shape=(jax.Shap...]
where the time goes in v2:
time: 21.5 us; the launch traced here: 21.3 us
  Pallas kernels  18.8 us (87%)
  local copies, waits for them, and re-layouts  1.86 us (9%)
  between operations  0.65 us (3%)
    pallas_call x1, Pallas kernels, local(): pl.pallas_call(functools.partial(kernel, nb, nc, ns), out_shape=(jax.Shap...  18.8 us
    unnamed x6, local copies, waits for them, and re-layouts  1.86 us

profile of v2, /device:TPU:0, one launch (start us, length us, event | category | flops | bytes accessed | tf_op | source)
XLA Modules:
  0.0 21.3 jit_solution(5445569663468769104)
XLA Ops:
  0.6 18.8 %shard_map.41 = (f32[1,256]{1,0:T(1,128)}, f32[1,256]{1,0:T(1,128)}) custom-call(bf16[256,128]{1,0:T(8,128)(2,1)} %f_ref.1, f32[1,256]{1,0:T(1,128)} %bitcast.3), custom_call_target="tpu_custom_call" | custom-call | tf_op jit(solution)/shard_map/pallas_call | solution.py:202
  19.4 0.0 copy-start.1
  19.4 0.7 %copy-done.1 = f32[1,256]{1,0:T(1,128)S(1)} copy-done((f32[1,256]{1,0:T(1,128)S(1)}, f32[1,256]{1,0:T(1,128)}, u32[]{:S(2)}) %copy-start.1) | copy-done | bytes 1048
  20.1 0.0 copy-start
  20.1 0.6 %copy.6 = f32[256]{0:T(256)} copy(f32[256]{0:T(256)S(1)} %bitcast.5) | data formatting | bytes 2048
  20.6 0.1 copy-done
  20.7 0.6 %copy.7 = f32[256]{0:T(256)} copy(f32[256]{0:T(256)S(1)} %bitcast.4) | data formatting | bytes 2048
Async XLA Ops:
  19.4 0.7 %copy-start.1 = (f32[1,256]{1,0:T(1,128)S(1)}, f32[1,256]{1,0:T(1,128)}, u32[]{:S(2)}) copy-start(f32[1,256]{1,0:T(1,128)} %get-tuple-element.4) | copy-start | bytes 3076
  20.1 0.6 %copy-start = (f32[1,256]{1,0:T(1,128)S(1)}, f32[1,256]{1,0:T(1,128)}, u32[]{:S(2)}) copy-start(f32[1,256]{1,0:T(1,128)} %get-tuple-element.5) | copy-start | bytes 3076

commit v3 on v2

--- a/solution.py
+++ b/solution.py
@@ -22,12 +22,17 @@
 
 
 def kernel(
-    nb, nc, ns, f_ref, v_ref, new_ref, mean_ref,
+    nb, nc, ns, f_hbm, v_hbm, new_ref, mean_ref,
+    f_ref, v_ref, load_sem,
     row_buf, col_buf, val_buf, unit, part, all_buf, own_sums,
     row_send, row_recv, col_send, col_recv, val_send, val_recv,
     all_send, all_recv, below_in, above_in,
 ):
     z, x, c = lax.axis_index("blk"), lax.axis_index("cols"), lax.axis_index("sub")
+    f_load = pltpu.make_async_copy(f_hbm, f_ref, load_sem.at[0])
+    v_load = pltpu.make_async_copy(v_hbm, v_ref, load_sem.at[1])
+    f_load.start()
+    v_load.start()
     rows, feats = f_ref.shape
     half = rows // ns
     points = rows * nb * nc
@@ -56,6 +61,9 @@
     beside = jnp.where(z >= 1, ns, 0) + jnp.where(z + 1 < nb, ns, 0)
     pl.semaphore_wait(barrier, len(plane) + beside)
 
+    f_load.wait()
+    v_load.wait()
+
     def remote(src, dst, send, recv, device):
         return pltpu.make_async_remote_copy(
             src_ref=src, dst_ref=dst, send_sem=send, recv_sem=recv,
@@ -81,6 +89,13 @@
         for e in range(ns):
             col_copy[nb - d, e].start()
         val_copy[nb - d].start()
+
+    for d, e in plane:
+        slot = ((nc - d) % nc, e)
+        row_copy[slot] = remote(
+            f_ref, row_buf.at[slot], row_send.at[slot], row_recv.at[slot], plane_id(d, e)
+        )
+        row_copy[slot].start()
 
     for k in ahead:
         @pl.when(z + k < nb)
@@ -107,14 +122,6 @@
                     )
             start_line(nb - k)
 
-        if k == 1:
-            for d, e in plane:
-                slot = ((nc - d) % nc, e)
-                row_copy[slot] = remote(
-                    f_ref, row_buf.at[slot], row_send.at[slot], row_recv.at[slot], plane_id(d, e)
-                )
-                row_copy[slot].start()
-
     for d in range(nc):
         for e in range(ns):
             if (d, e) in row_copy:
@@ -152,7 +159,7 @@
         part[i:i + 1, :] = weighted[:, i * 128:(i + 1) * 128]
         part[tiles + i:tiles + i + 1, :] = degree[:, i * 128:(i + 1) * 128]
 
-    for dz in ahead + [0]:
+    for dz in [0] + ahead:
         for d in range(nc):
             for e in range(ns):
                 if (dz, d, e) == (0, 0, 0):
@@ -187,8 +194,9 @@
     for i in range(rows // 128):
         lanes = slice(i * 128, (i + 1) * 128)
         first = x * (rows // 128) + i
-        new_ref[:, lanes] = own_sums[pl.ds(first, 1), :] / mean
-        mean_ref[:, lanes] = own_sums[pl.ds(tiles + first, 1), :] / points
+        new_ref[0:1, lanes] = own_sums[pl.ds(first, 1), :]
+        new_ref[1:2, lanes] = own_sums[pl.ds(tiles + first, 1), :]
+    mean_ref[...] = jnp.broadcast_to(mean, mean_ref.shape)
     for copy in all_copy.values():
         copy.wait_send()
 
@@ -202,12 +210,15 @@
     new, mean = pl.pallas_call(
         functools.partial(kernel, nb, nc, ns),
         out_shape=(
-            jax.ShapeDtypeStruct((1, rows), jnp.float32),
-            jax.ShapeDtypeStruct((1, rows), jnp.float32),
+            jax.ShapeDtypeStruct((2, rows), jnp.float32),
+            jax.ShapeDtypeStruct((1, 128), jnp.float32),
         ),
-        in_specs=[vmem, vmem],
+        in_specs=[pl.BlockSpec(memory_space=pl.ANY)] * 2,
         out_specs=(vmem, vmem),
         scratch_shapes=[
+            pltpu.VMEM((rows, feats), jnp.bfloat16),
+            pltpu.VMEM((1, rows), jnp.float32),
+            dma((2,)),
             pltpu.VMEM((nc, ns, rows, feats), jnp.bfloat16),
             pltpu.VMEM((nb, ns, half, feats), jnp.bfloat16),
             pltpu.VMEM((nb, 1, half), jnp.float32),
@@ -223,7 +234,8 @@
         ],
         compiler_params=pltpu.CompilerParams(collective_id=0, has_side_effects=True),
     )(features, vector.reshape(1, rows))
-    return new.reshape(rows), mean.reshape(rows)
+    points = rows * nb * nc
+    return new[0] / mean[0, 0], new[1] / points
 
 
 def solution(mesh):

time: 21.5 us -> 20.1 us (0.935)
  local copies, waits for them, and re-layouts: 1.86 us -> 0.64 us
  Pallas kernels: 18.8 us -> 18 us
  other arithmetic: 0 us -> 0.6 us
    unnamed x6 -> x4, local copies, waits for them, and re-layouts: 1.86 us -> 0.64 us
    pallas_call x1, Pallas kernels: 18.8 us -> 18 us  [local(): pl.pallas_call(functools.partial(kernel, nb, nc, ns), out_shape=(jax.Shap...]
    div x0 -> x1, other arithmetic: none -> 0.6 us  [local(): return (new[0] / mean[0, 0], new[1] / points)]
where the time goes in v3:
time: 20.1 us; the launch traced here: 19.9 us
  Pallas kernels  18 us (90%)
  between operations  0.65 us (3%)
  local copies, waits for them, and re-layouts  0.64 us (3%)
  other arithmetic  0.6 us (3%)
    pallas_call x1, Pallas kernels, local(): pl.pallas_call(functools.partial(kernel, nb, nc, ns), out_shape=(jax.Shap...  18 us
    unnamed x4, local copies, waits for them, and re-layouts  0.64 us
    div x1, other arithmetic, local(): return (new[0] / mean[0, 0], new[1] / points)  0.6 us

profile of v3, /device:TPU:0, one launch (start us, length us, event | category | flops | bytes accessed | tf_op | source)
XLA Modules:
  0.0 19.9 jit_solution(7582285145723772999)
XLA Ops:
  0.6 18.0 %shard_map.41 = (f32[2,256]{1,0:T(2,128)}, f32[1,128]{1,0:T(1,128)}) custom-call(bf16[256,128]{1,0:T(8,128)(2,1)} %f_hbm.1, f32[1,256]{1,0:T(1,128)} %bitcast.5), custom_call_target="tpu_custom_call" | custom-call | tf_op jit(solution)/shard_map/pallas_call | solution.py:210
  18.6 0.0 copy-start
  18.7 0.0 copy-start.1
  18.7 0.6 %copy-done = f32[2,256]{1,0:T(2,128)S(1)} copy-done((f32[2,256]{1,0:T(2,128)S(1)}, f32[2,256]{1,0:T(2,128)}, u32[]{:S(2)}) %copy-start) | copy-done | bytes 2072
  19.3 0.0 copy-done.1
  19.3 0.6 %slice_multiply_fusion = (f32[1,256]{1,0:T(1,128)}, f32[1,256]{1,0:T(1,128)}) fusion(f32[2,256]{1,0:T(2,128)S(1)} %copy-done, f32[]{:T(128)S(1)} %bitcast.8), kind=kLoop, calls=%fused_computation | loop fusion | flops 512 | bytes 4100 | tf_op jit(solution)/shard_map/div | solution.py:238
Async XLA Ops:
  18.6 0.7 %copy-start = (f32[2,256]{1,0:T(2,128)S(1)}, f32[2,256]{1,0:T(2,128)}, u32[]{:S(2)}) copy-start(f32[2,256]{1,0:T(2,128)} %get-tuple-element.4) | copy-start | bytes 6148
  18.7 0.7 %copy-start.1 = (f32[1,128]{1,0:T(1,128)S(1)}, f32[1,128]{1,0:T(1,128)}, u32[]{:S(2)}) copy-start(f32[1,128]{1,0:T(1,128)} %get-tuple-element.5) | copy-start | bytes 1540

commit v4 on v3

--- a/solution.py
+++ b/solution.py
@@ -22,7 +22,7 @@
 
 
 def kernel(
-    nb, nc, ns, f_hbm, v_hbm, new_ref, mean_ref,
+    nb, nc, ns, f_hbm, v_hbm, new_ref,
     f_ref, v_ref, load_sem,
     row_buf, col_buf, val_buf, unit, part, all_buf, own_sums,
     row_send, row_recv, col_send, col_recv, val_send, val_recv,
@@ -196,7 +196,7 @@
         first = x * (rows // 128) + i
         new_ref[0:1, lanes] = own_sums[pl.ds(first, 1), :]
         new_ref[1:2, lanes] = own_sums[pl.ds(tiles + first, 1), :]
-    mean_ref[...] = jnp.broadcast_to(mean, mean_ref.shape)
+    new_ref[2:3, :] = jnp.broadcast_to(mean, (1, rows))
     for copy in all_copy.values():
         copy.wait_send()
 
@@ -207,14 +207,11 @@
     tiles = 2 * nc * rows // 128
     dma = pltpu.SemaphoreType.DMA
     vmem = pl.BlockSpec(memory_space=pltpu.VMEM)
-    new, mean = pl.pallas_call(
+    sums = pl.pallas_call(
         functools.partial(kernel, nb, nc, ns),
-        out_shape=(
-            jax.ShapeDtypeStruct((2, rows), jnp.float32),
-            jax.ShapeDtypeStruct((1, 128), jnp.float32),
-        ),
+        out_shape=pltpu.VMEM((3, rows), jnp.float32),
         in_specs=[pl.BlockSpec(memory_space=pl.ANY)] * 2,
-        out_specs=(vmem, vmem),
+        out_specs=vmem,
         scratch_shapes=[
             pltpu.VMEM((rows, feats), jnp.bfloat16),
             pltpu.VMEM((1, rows), jnp.float32),
@@ -235,7 +232,7 @@
         compiler_params=pltpu.CompilerParams(collective_id=0, has_side_effects=True),
     )(features, vector.reshape(1, rows))
     points = rows * nb * nc
-    return new[0] / mean[0, 0], new[1] / points
+    return sums[0] / sums[2], sums[1] / points
 
 
 def solution(mesh):

time: 20.1 us -> 18.8 us (0.935)
  local copies, waits for them, and re-layouts: 0.64 us -> 0 us
  Pallas kernels: 18 us -> 17.4 us
    unnamed x4 -> x0, local copies, waits for them, and re-layouts: 0.64 us -> none
    pallas_call x1, Pallas kernels: 18 us -> 17.4 us  [local(): pl.pallas_call(functools.partial(kernel, nb, nc, ns), out_shape=pltpu.VME...]
where the time goes in v4:
time: 18.8 us; the launch traced here: 18.7 us
  Pallas kernels  17.4 us (93%)
  between operations  0.64 us (3%)
  other arithmetic  0.57 us (3%)
    pallas_call x1, Pallas kernels, local(): pl.pallas_call(functools.partial(kernel, nb, nc, ns), out_shape=pltpu.VME...  17.4 us
    div x1, other arithmetic, local(): return (sums[0] / sums[2], sums[1] / points)  0.57 us

profile of v4, /device:TPU:0, one launch (start us, length us, event | category | flops | bytes accessed | tf_op | source)
XLA Modules:
  0.0 18.7 jit_solution(13251735446064120590)
XLA Ops:
  0.6 17.4 %shard_map.41 = f32[3,256]{1,0:T(4,128)S(1)} custom-call(bf16[256,128]{1,0:T(8,128)(2,1)} %f_hbm.1, f32[1,256]{1,0:T(1,128)} %bitcast.3), custom_call_target="tpu_custom_call" | custom-call | tf_op jit(solution)/shard_map/pallas_call | solution.py:210
  18.1 0.6 %slice_multiply_fusion = (f32[1,256]{1,0:T(1,128)}, f32[1,256]{1,0:T(1,128)}) fusion(f32[3,256]{1,0:T(4,128)S(1)} %shard_map.41), kind=kLoop, calls=%fused_computation | loop fusion | flops 512 | bytes 5120 | tf_op jit(solution)/shard_map/div | solution.py:235

commit v5 on v4

--- a/solution.py
+++ b/solution.py
@@ -159,7 +159,7 @@
         part[i:i + 1, :] = weighted[:, i * 128:(i + 1) * 128]
         part[tiles + i:tiles + i + 1, :] = degree[:, i * 128:(i + 1) * 128]
 
-    for dz in [0] + ahead:
+    for dz in range(nb):
         for d in range(nc):
             for e in range(ns):
                 if (dz, d, e) == (0, 0, 0):
@@ -169,7 +169,22 @@
                     part, all_buf.at[slot], all_send.at[slot], all_recv.at[slot],
                     full_id(dz, d, e),
                 )
-                all_copy[slot].start()
+
+    def spread(dz):
+        for d in range(nc):
+            for e in range(ns):
+                if (dz, d, e) != (0, 0, 0):
+                    all_copy[(nb - dz) % nb, (nc - d) % nc, e].start()
+
+    for k in reversed(ahead):
+        @pl.when(z + k < nb)
+        def _():
+            spread(k)
+
+        @pl.when(z >= k)
+        def _():
+            spread(nb - k)
+    spread(0)
     for copies in (row_copy, col_copy, val_copy):
         for copy in copies.values():
             copy.wait_send()

time: 18.8 us -> 18.8 us (level)
  no operation moved by 1% of the time
where the time goes in v5:
time: 18.8 us; the launch traced here: 18.7 us
  Pallas kernels  17.5 us (93%)
  between operations  0.64 us (3%)
  other arithmetic  0.57 us (3%)
    pallas_call x1, Pallas kernels, local(): pl.pallas_call(functools.partial(kernel, nb, nc, ns), out_shape=pltpu.VME...  17.5 us
    div x1, other arithmetic, local(): return (sums[0] / sums[2], sums[1] / points)  0.57 us

profile of v5, /device:TPU:0, one launch (start us, length us, event | category | flops | bytes accessed | tf_op | source)
XLA Modules:
  0.0 18.7 jit_solution(8266796188883563101)
XLA Ops:
  0.6 17.5 %shard_map.41 = f32[3,256]{1,0:T(4,128)S(1)} custom-call(bf16[256,128]{1,0:T(8,128)(2,1)} %f_hbm.1, f32[1,256]{1,0:T(1,128)} %bitcast.3), custom_call_target="tpu_custom_call" | custom-call | tf_op jit(solution)/shard_map/pallas_call | solution.py:225
  18.1 0.6 %slice_multiply_fusion = (f32[1,256]{1,0:T(1,128)}, f32[1,256]{1,0:T(1,128)}) fusion(f32[3,256]{1,0:T(4,128)S(1)} %shard_map.41), kind=kLoop, calls=%fused_computation | loop fusion | flops 512 | bytes 5120 | tf_op jit(solution)/shard_map/div | solution.py:250
